TPU v7x, 32 devices: a whole 2x2x4 slice. The times are simulated.
32 devices in a mesh: fsdp: 2 (over x), ctx: 4 (over y, core), tp: 4 (over z).
Axes of the slice: x: 2, y: 2, z: 4, core: 2. Of those that a mesh axis runs over, the one named last changes fastest.
Arguments:
- inputs: bfloat16 [4, 1024, 2048], P('fsdp', 'ctx'), may hold values from -6 to 6
- prefix: int32 [4], P('fsdp'), may hold values from 102 to 512, as said below
- expert_ids: int32 [4, 1024, 8], P('fsdp', 'ctx'), may hold values from 0 to 15, all different within a row
- norm_gains: bfloat16 [4, 2048], P(None, ('fsdp', 'ctx')), may hold values from 0.5 to 1.5
- qkv_weight: bfloat16 [3, 2048, 2048], P(None, ('fsdp', 'ctx'), 'tp'), may hold values from -0.125 to 0.125
- out_weight: bfloat16 [2048, 2048], P(('fsdp', 'ctx'), 'tp'), may hold values from -1 to 1
- router_weight: bfloat16 [2048, 16], P(('fsdp', 'ctx')), may hold values from -0.0625 to 0.0625
- gate_up_weight: bfloat16 [16, 2, 2048, 1024], P(None, None, ('fsdp', 'ctx'), 'tp'), may hold values from -0.125 to 0.125
- down_weight: bfloat16 [16, 2048, 1024], P(None, ('fsdp', 'ctx'), 'tp'), may hold values from -1.5 to 1.5
- cotangent: bfloat16 [4, 1024, 2048], P('fsdp', 'ctx'), may hold values from -6 to 6
Outputs:
- outputs: bfloat16 [4, 1024, 2048], P('fsdp', 'ctx')
- grad_inputs: bfloat16 [4, 1024, 2048], P('fsdp', 'ctx')
- grad_norm_gains: float32 [4, 2048], P(None, ('fsdp', 'ctx'))
- grad_qkv_weight: float32 [3, 2048, 2048], P(None, ('fsdp', 'ctx'), 'tp')
- grad_out_weight: float32 [2048, 2048], P(('fsdp', 'ctx'), 'tp')
- grad_router_weight: float32 [2048, 16], P(('fsdp', 'ctx'))
- grad_gate_up_weight: float32 [16, 2, 2048, 1024], P(None, None, ('fsdp', 'ctx'), 'tp')
- grad_down_weight: float32 [16, 2048, 1024], P(None, ('fsdp', 'ctx'), 'tp')
Inputs may be any that keep to these rules, and one draw needn't show every extreme that they name: `expert_ids`: each token names 8 different experts. Some sequence has the shortest and some the longest allowed prefix.
All inputs are finite; a program needn't handle non-finite values.
Results may differ from a plain program's by a relative error of at most 0.017.
Values may be sent and summed in bfloat16 or wider, within the bound.
No kernel may reach another device: no remote copies, remote signals or barrier semaphores. Data moves between devices by JAX's collectives and lax.ppermute only.
A program may use at most 384 MiB of HBM per device.

v0:
```python
import jax
import jax.numpy as jnp
from jax import lax
from jax.sharding import PartitionSpec as P

HEAD_DIM = 128
EPSILON = 1e-05
THETA = 10000.0


def rotary_tables(positions, head_width):
    halves = jnp.arange(0, head_width, 2).astype(jnp.float32) / head_width
    inverse = 1.0 / THETA**halves
    angles = positions.astype(jnp.float32)[:, None] * inverse[None, :]
    return (jnp.cos(angles), jnp.sin(angles))


def rotate(values, cosine, sine):
    half = values.shape[-1] // 2
    first = values[..., :half]
    second = values[..., half:]
    cosine = cosine[:, None, :]
    sine = sine[:, None, :]
    return jnp.concatenate([first * cosine - second * sine, second * cosine + first * sine], -1)


def unrotate(grads, cosine, sine):
    half = grads.shape[-1] // 2
    first = grads[..., :half]
    second = grads[..., half:]
    cosine = cosine[:, None, :]
    sine = sine[:, None, :]
    return jnp.concatenate([first * cosine + second * sine, second * cosine - first * sine], -1)


def contract_rows(left, right):
    return lax.dot_general(
        left, right, (((0,), (0,)), ((), ())), preferred_element_type=jnp.float32
    )


def contract_last(left, right):
    return lax.dot_general(
        left, right, (((1,), (1,)), ((), ())), preferred_element_type=jnp.float32
    )


def body(
    inputs,
    prefix,
    expert_ids,
    norm_gains,
    qkv_weight,
    out_weight,
    router_weight,
    gate_up_weight,
    down_weight,
    cotangent,
):
    sequences, local_len, width = inputs.shape
    tokens = sequences * local_len
    full_len = local_len * lax.axis_size("ctx")
    gains_low, qkv_full, out_full = (
        lax.all_gather(norm_gains, ("fsdp", "ctx"), axis=1, tiled=True),
        lax.all_gather(qkv_weight, ("fsdp", "ctx"), axis=1, tiled=True),
        lax.all_gather(out_weight, ("fsdp", "ctx"), axis=0, tiled=True),
    )
    gains = gains_low.astype(jnp.float32)
    local_width = qkv_full.shape[2]
    head_width = HEAD_DIM
    local_heads = local_width // head_width
    head_scale = head_width ** (-0.5)
    column_start = lax.axis_index("tp") * local_width
    query_gain = lax.dynamic_slice_in_dim(gains[2], column_start, local_width)
    key_gain = lax.dynamic_slice_in_dim(gains[3], column_start, local_width)
    residual = inputs.reshape(tokens, width).astype(jnp.float32)
    scale_one = lax.rsqrt(jnp.mean(residual * residual, -1, keepdims=True) + EPSILON)
    normal_one = residual * scale_one
    normed_one = (normal_one * gains[0]).astype(jnp.bfloat16)
    projected = jnp.einsum("td,cde->cte", normed_one, qkv_full, preferred_element_type=jnp.float32)
    query_raw = projected[0]
    key_raw = projected[1]
    value_raw = projected[2]
    query_squares, key_squares = lax.psum(
        (jnp.sum(query_raw * query_raw, -1), jnp.sum(key_raw * key_raw, -1)), "tp"
    )
    query_scale = lax.rsqrt(query_squares / width + EPSILON)[:, None]
    key_scale = lax.rsqrt(key_squares / width + EPSILON)[:, None]
    query_hat = query_raw * query_scale
    key_hat = key_raw * key_scale
    positions = lax.axis_index("ctx") * local_len + jnp.arange(local_len, dtype=jnp.int32)
    cosine, sine = rotary_tables(positions, head_width)
    head_shape = (sequences, local_len, local_heads, head_width)
    queries = rotate((query_hat * query_gain).reshape(head_shape), cosine, sine).astype(
        jnp.bfloat16
    )
    keys_local = rotate((key_hat * key_gain).reshape(head_shape), cosine, sine).astype(jnp.bfloat16)
    values_local = value_raw.reshape(head_shape).astype(jnp.bfloat16)
    all_keys, all_values = (
        lax.all_gather(keys_local, "ctx", axis=1, tiled=True),
        lax.all_gather(values_local, "ctx", axis=1, tiled=True),
    )
    key_places = jnp.arange(full_len, dtype=jnp.int32)
    visible = (key_places[None, None, :] <= positions[None, :, None]) | (
        key_places[None, None, :] < prefix[:, None, None]
    )
    visible = visible[:, None]
    scores = (
        jnp.einsum("sqhd,skhd->shqk", queries, all_keys, preferred_element_type=jnp.float32)
        * head_scale
    )
    masked = jnp.where(visible, scores, -1e30)
    maxima = jnp.max(masked, -1, keepdims=True)
    expo = jnp.exp(masked - maxima)
    totals = jnp.sum(expo, -1, keepdims=True)
    probs = expo / totals
    log_total = maxima + jnp.log(totals)
    heads_out = jnp.einsum(
        "shqk,skhd->sqhd",
        probs.astype(jnp.bfloat16),
        all_values,
        preferred_element_type=jnp.float32,
    )
    heads_out = heads_out.astype(jnp.bfloat16).reshape(tokens, local_width)
    attn_total = lax.psum(contract_last(heads_out, out_full), "tp")
    mid = residual + attn_total
    scale_two = lax.rsqrt(jnp.mean(mid * mid, -1, keepdims=True) + EPSILON)
    normal_two = mid * scale_two
    normed_two = (normal_two * gains[1]).astype(jnp.bfloat16)
    gate_up_full, down_full, router_full = (
        lax.all_gather(gate_up_weight, ("fsdp", "ctx"), axis=2, tiled=True),
        lax.all_gather(down_weight, ("fsdp", "ctx"), axis=1, tiled=True),
        lax.all_gather(router_weight, ("fsdp", "ctx"), axis=0, tiled=True),
    )
    expert_count = router_full.shape[1]
    logits = jnp.dot(normed_two, router_full, preferred_element_type=jnp.float32)
    router_probs = jax.nn.softmax(logits, -1)
    chosen = jnp.sum(
        (
            expert_ids.reshape(tokens, -1)[:, :, None]
            == jnp.arange(expert_count, dtype=jnp.int32)[None, None, :]
        ).astype(jnp.float32),
        1,
    )
    gates = router_probs * chosen

    def expert_forward(carry, entries):
        pair_weights, down_one, gate_one = entries
        activations = jnp.einsum(
            "td,cdf->ctf", normed_two, pair_weights, preferred_element_type=jnp.float32
        )
        hidden = (gate_one[:, None] * jax.nn.silu(activations[0]) * activations[1]).astype(
            jnp.bfloat16
        )
        return (carry + contract_last(hidden, down_one), activations)

    moe_part, kept_activations = lax.scan(
        expert_forward, jnp.zeros((tokens, width), jnp.float32), (gate_up_full, down_full, gates.T)
    )
    moe_total = lax.psum(moe_part.astype(jnp.bfloat16), "tp").astype(jnp.float32)
    outputs = (mid + moe_total).astype(jnp.bfloat16).reshape(inputs.shape)
    grad_out = cotangent.reshape(tokens, width)
    grad_float = grad_out.astype(jnp.float32)
    gate_up_back, down_back, router_back = (
        lax.all_gather(gate_up_weight, ("fsdp", "ctx"), axis=2, tiled=True),
        lax.all_gather(down_weight, ("fsdp", "ctx"), axis=1, tiled=True),
        lax.all_gather(router_weight, ("fsdp", "ctx"), axis=0, tiled=True),
    )

    def expert_backward(carry, entries):
        pair_weights, down_one, gate_one, activations = entries
        grad_hidden = jnp.dot(grad_out, down_one, preferred_element_type=jnp.float32)
        sigma = jax.nn.sigmoid(activations[0])
        swish = jax.nn.silu(activations[0])
        hidden = (gate_one[:, None] * swish * activations[1]).astype(jnp.bfloat16)
        grad_down = contract_rows(grad_out, hidden)
        grad_gate = jnp.sum(grad_hidden * swish * activations[1], -1)
        grad_inner = grad_hidden * gate_one[:, None]
        grad_act_gate = grad_inner * activations[1] * sigma * (1.0 + activations[0] * (1.0 - sigma))
        grad_act_up = grad_inner * swish
        grad_acts = jnp.stack([grad_act_gate, grad_act_up]).astype(jnp.bfloat16)
        grad_pair = jnp.einsum(
            "td,ctf->cdf", normed_two, grad_acts, preferred_element_type=jnp.float32
        )
        carry = carry + jnp.einsum(
            "ctf,cdf->td", grad_acts, pair_weights, preferred_element_type=jnp.float32
        )
        return (carry, (grad_pair, grad_down, grad_gate))

    back_inputs = (gate_up_back, down_back, gates.T, kept_activations)
    zero_rows = jnp.zeros((tokens, width), jnp.float32)
    expert_part, (grad_gate_up, grad_down_all, grad_gates) = lax.scan(
        expert_backward, zero_rows, back_inputs
    )
    expert_grad_norm, gate_grads = lax.psum((expert_part, grad_gates.T), "tp")
    masked_grads = gate_grads * chosen
    grad_logits = (
        router_probs * (masked_grads - jnp.sum(router_probs * masked_grads, -1, keepdims=True))
    ).astype(jnp.bfloat16)
    grad_router = contract_rows(normed_two, grad_logits)
    grad_normed_two = expert_grad_norm + contract_last(grad_logits, router_back)
    owned_gate_up, owned_down, owned_router = (
        lax.psum_scatter(grad_gate_up, ("fsdp", "ctx"), scatter_dimension=2, tiled=True),
        lax.psum_scatter(grad_down_all, ("fsdp", "ctx"), scatter_dimension=1, tiled=True),
        lax.psum_scatter(grad_router, ("fsdp", "ctx"), scatter_dimension=0, tiled=True),
    )
    weighted_two = grad_normed_two * gains[1]
    grad_mid = grad_float + scale_two * (
        weighted_two - normal_two * jnp.mean(weighted_two * normal_two, -1, keepdims=True)
    )
    gain_two_grad = jnp.sum(grad_normed_two * normal_two, 0)
    grad_mid_low = grad_mid.astype(jnp.bfloat16)
    grad_out_weight = contract_rows(grad_mid_low, heads_out)
    grad_heads = (
        jnp.dot(grad_mid_low, out_full, preferred_element_type=jnp.float32)
        .astype(jnp.bfloat16)
        .reshape(head_shape)
    )
    scores_again = (
        jnp.einsum("sqhd,skhd->shqk", queries, all_keys, preferred_element_type=jnp.float32)
        * head_scale
    )
    probs_again = jnp.exp(jnp.where(visible, scores_again, -1e30) - log_total)
    grad_probs = jnp.einsum(
        "sqhd,skhd->shqk", grad_heads, all_values, preferred_element_type=jnp.float32
    )
    inner_sums = jnp.sum(probs_again * grad_probs, -1, keepdims=True)
    grad_scores = (probs_again * (grad_probs - inner_sums)).astype(jnp.bfloat16)
    grad_queries = (
        jnp.einsum("shqk,skhd->sqhd", grad_scores, all_keys, preferred_element_type=jnp.float32)
        * head_scale
    )
    grad_keys_all = (
        jnp.einsum("shqk,sqhd->skhd", grad_scores, queries, preferred_element_type=jnp.float32)
        * head_scale
    )
    grad_values_all = jnp.einsum(
        "shqk,sqhd->skhd",
        probs_again.astype(jnp.bfloat16),
        grad_heads,
        preferred_element_type=jnp.float32,
    )
    grad_keys, grad_values = (
        lax.psum_scatter(grad_keys_all, "ctx", scatter_dimension=1, tiled=True),
        lax.psum_scatter(grad_values_all, "ctx", scatter_dimension=1, tiled=True),
    )
    grad_query_hat = unrotate(grad_queries, cosine, sine).reshape(tokens, local_width)
    grad_key_hat = unrotate(grad_keys, cosine, sine).reshape(tokens, local_width)
    weighted_query = grad_query_hat * query_gain
    weighted_key = grad_key_hat * key_gain
    query_inner, key_inner = lax.psum(
        (jnp.sum(weighted_query * query_hat, -1), jnp.sum(weighted_key * key_hat, -1)), "tp"
    )
    grad_query_raw = (
        query_scale * (weighted_query - query_hat * (query_inner / width)[:, None])
    ).astype(jnp.bfloat16)
    grad_key_raw = (key_scale * (weighted_key - key_hat * (key_inner / width)[:, None])).astype(
        jnp.bfloat16
    )
    grad_value_raw = grad_values.reshape(tokens, local_width).astype(jnp.bfloat16)
    grad_projected = jnp.stack([grad_query_raw, grad_key_raw, grad_value_raw])
    grad_qkv = jnp.einsum(
        "td,cte->cde", normed_one, grad_projected, preferred_element_type=jnp.float32
    )
    grad_normed_part = jnp.einsum(
        "cte,cde->td", grad_projected, qkv_full, preferred_element_type=jnp.float32
    )
    local_gain_grads = jnp.stack(
        [jnp.sum(grad_query_hat * query_hat, 0), jnp.sum(grad_key_hat * key_hat, 0)]
    )
    placed_gains = lax.dynamic_update_slice_in_dim(
        jnp.zeros((2, width), jnp.float32), local_gain_grads, column_start, 1
    )
    grad_normed_one, qk_gain_grads = lax.psum((grad_normed_part, placed_gains), "tp")
    weighted_one = grad_normed_one * gains[0]
    grad_input = grad_mid + scale_one * (
        weighted_one - normal_one * jnp.mean(weighted_one * normal_one, -1, keepdims=True)
    )
    gain_one_grad = jnp.sum(grad_normed_one * normal_one, 0)
    grad_gains = jnp.stack([gain_one_grad, gain_two_grad, qk_gain_grads[0], qk_gain_grads[1]])
    owned_gains, owned_qkv, owned_out = (
        lax.psum_scatter(grad_gains, ("fsdp", "ctx"), scatter_dimension=1, tiled=True),
        lax.psum_scatter(grad_qkv, ("fsdp", "ctx"), scatter_dimension=1, tiled=True),
        lax.psum_scatter(grad_out_weight, ("fsdp", "ctx"), scatter_dimension=0, tiled=True),
    )
    return (
        outputs,
        grad_input.astype(jnp.bfloat16).reshape(inputs.shape),
        owned_gains,
        owned_qkv,
        owned_out,
        owned_router,
        owned_gate_up,
        owned_down,
    )


def solution(mesh):
    return jax.shard_map(
        body,
        mesh=mesh,
        in_specs=(
            P("fsdp", "ctx", None),
            P("fsdp"),
            P("fsdp", "ctx", None),
            P(None, ("fsdp", "ctx")),
            P(None, ("fsdp", "ctx"), "tp"),
            P(("fsdp", "ctx"), "tp"),
            P(("fsdp", "ctx"), None),
            P(None, None, ("fsdp", "ctx"), "tp"),
            P(None, ("fsdp", "ctx"), "tp"),
            P("fsdp", "ctx", None),
        ),
        out_specs=(
            P("fsdp", "ctx", None),
            P("fsdp", "ctx", None),
            P(None, ("fsdp", "ctx")),
            P(None, ("fsdp", "ctx"), "tp"),
            P(("fsdp", "ctx"), "tp"),
            P(("fsdp", "ctx"), None),
            P(None, None, ("fsdp", "ctx"), "tp"),
            P(None, ("fsdp", "ctx"), "tp"),
        ),
        check_vma=False,
    )
```

profile of v0, /device:TPU:0, one launch (start us, length us, event | category | flops | bytes accessed | tf_op | source)
XLA Modules:
  0.0 2617.0 jit_solution(943007271589671076)
XLA Ops:
  11.9 10.4 all_gather.27
  24.7 35.1 %all-gather.7.cloned.1.call-done = bf16[3,2048,512]{1,2,0:T(8,128)(2,1)} async-done(((bf16[3,256,512]{1,2,0:T(8,128)(2,1)}), bf16[3,2048,512]{1,2,0:T(8,128)(2,1)}) %all-gather.7.cloned.1.call-update) | async-done | bytes 6291472 | tf_op jit(solution)/shard_map/all_gather | solution.py:65
  69.0 11.7 all-reduce.1
  101.0 11.4 all-gather.11.cloned.1.call-done
  121.4 16.0 all-gather.9.cloned.1.call-done
  143.6 23.5 all-gather.13.cloned.1.call-done
  182.7 144.4 %all-reduce.7.cloned.1.call-done = f32[512,2048]{1,0:T(8,128)} async-done(((f32[512,2048]{1,0:T(8,128)}), f32[512,2048]{1,0:T(8,128)}) %all-reduce.7.cloned.1.call-update) | async-done | bytes 4194320 | tf_op jit(solution)/shard_map/psum | solution.py:125
  332.0 86.0 %all-gather.17.cloned.1.call-done = bf16[16,2048,256]{2,1,0:T(8,128)(2,1)} async-done(((bf16[16,256,256]{2,1,0:T(8,128)(2,1)}), bf16[16,2048,256]{2,1,0:T(8,128)(2,1)}) %all-gather.17.cloned.1.call-update) | async-done | bytes 16777232 | tf_op jit(solution)/shard_map/all_gather | solution.py:132
  418.0 162.9 %all-gather.15.cloned.1.call-done = bf16[16,2,2048,256]{3,2,1,0:T(8,128)(2,1)} async-done(((bf16[16,2,256,256]{3,2,1,0:T(8,128)(2,1)}), bf16[16,2,2048,256]{3,2,1,0:T(8,128)(2,1)}) %all-gather.15.cloned.1.call-update) | async-done | bytes 33554448 | tf_op jit(solution)/shard_map/all_gather | solution.py:131
  580.9 145.9 %while.30 = (s32[]{:T(128)}, f32[512,2048]{1,0:T(8,128)}, f32[16,2,512,256]{2,3,1,0:T(8,128)}, f32[16,512]{1,0:T(8,128)S(1)}, bf16[16,2,2048,256]{3,2,1,0:T(8,12...) while((s32[]{:T(128)}, f32[512,2048]{1,0:T(8,128)}, ...), condition=%wide.region_13.14_spmd.clone, body=%wide.region_12.13_spmd.clone.sunk | while | flops 1613627392 | bytes 50338988 | solution.py:157
  726.8 503.8 %while.31 = (s32[]{:T(128)}, f32[512,2048]{1,0:T(8,128)}, f32[16,2,2048,256]{3,2,1,0:T(8,128)}, f32[16,2048,256]{2,1,0:T(8,128)}, f32[16,512]{1,0:T(8,128)S(1)},...) while((s32[]{:T(128)}, f32[512,2048]{1,0:T(8,128)}, ...), condition=%wide.region_17.18_spmd.clone, body=%wide.region_15.17_spmd.clone.sunk | while | flops 3226992128 | bytes 86523664 | solution.py:192
  1234.6 20.3 psum.75
  1255.0 131.8 %all-reduce.11.cloned.1.call-done = f32[512,2048]{1,0:T(8,128)} async-done(((f32[512,2048]{1,0:T(8,128)}), f32[512,2048]{1,0:T(8,128)}) %all-reduce.11.cloned.1.call-update) | async-done | bytes 4194320 | tf_op jit(solution)/shard_map/psum | solution.py:195
  1393.4 81.8 %all-reduce.9.cloned.1.call-done = bf16[512,2048]{1,0:T(8,128)(2,1)} async-done(((bf16[512,2048]{1,0:T(8,128)(2,1)}), bf16[512,2048]{1,0:T(8,128)(2,1)}) %all-reduce.9.cloned.1.call-update) | async-done | bytes 2097168 | tf_op jit(solution)/shard_map/psum | solution.py:160
  1514.6 21.7 reduce-scatter.13.cloned.1.call-done
  1541.1 42.3 %reduce-scatter.11.cloned.1.call-done = f32[2,256,4,128]{3,1,2,0:T(8,128)} async-done(((f32[2,1024,4,128]{3,1,2,0:T(8,128)}), f32[2,256,4,128]{3,1,2,0:T(8,128)}) %reduce-scatter.11.cloned.1.call-update) | async-done | bytes 1048592 | tf_op jit(solution)/shard_map/reduce_scatter | solution.py:244
  1601.3 19.0 all-reduce
  1631.5 152.3 %all-reduce.13.cloned.1.call-done = f32[512,2048]{1,0:T(8,128)} async-done(((f32[512,2048]{1,0:T(8,128)}), f32[512,2048]{1,0:T(8,128)}) %all-reduce.13.cloned.1.call-update) | async-done | bytes 4194320 | tf_op jit(solution)/shard_map/psum | solution.py:274
  1814.3 10.1 reduce-scatter.25.cloned.1.call-done
  1826.0 94.2 %reduce-scatter.15.cloned.1.call-done = f32[3,256,512]{1,2,0:T(8,128)} async-done(((f32[3,2048,512]{1,2,0:T(8,128)}), f32[3,256,512]{1,2,0:T(8,128)}) %reduce-scatter.15.cloned.1.call-update) | async-done | bytes 1572880 | tf_op jit(solution)/shard_map/reduce_scatter | solution.py:283
  1923.2 33.8 %reduce-scatter.19.cloned.1.call-done = f32[256,16]{0,1:T(8,128)} async-done(((f32[2048,16]{0,1:T(8,128)}), f32[256,16]{0,1:T(8,128)}) %reduce-scatter.19.cloned.1.call-update) | async-done | bytes 16400 | tf_op jit(solution)/shard_map/reduce_scatter | solution.py:205
  1957.0 55.5 %reduce-scatter.17.cloned.1.call-done = f32[256,512]{1,0:T(8,128)} async-done(((f32[2048,512]{1,0:T(8,128)}), f32[256,512]{1,0:T(8,128)}) %reduce-scatter.17.cloned.1.call-update) | async-done | bytes 524304 | tf_op jit(solution)/shard_map/reduce_scatter | solution.py:284
  2012.5 209.3 %reduce-scatter.23.cloned.1.call-done = f32[16,256,256]{2,1,0:T(8,128)} async-done(((f32[16,2048,256]{2,1,0:T(8,128)}), f32[16,256,256]{2,1,0:T(8,128)}) %reduce-scatter.23.cloned.1.call-update) | async-done | bytes 4194320 | tf_op jit(solution)/shard_map/reduce_scatter | solution.py:204
  2221.8 388.2 %reduce-scatter.21.cloned.1.call-done = f32[16,2,256,256]{3,2,1,0:T(8,128)} async-done(((f32[16,2,2048,256]{3,2,1,0:T(8,128)}), f32[16,2,256,256]{3,2,1,0:T(8,128)}) %reduce-scatter.21.cloned.1.call-update) | async-done | bytes 8388624 | tf_op jit(solution)/shard_map/reduce_scatter | solution.py:203
  (572 shorter events, 839.3 us)
Async XLA Ops:
  7.2 52.7 %all-gather.7.cloned.1.call-start = ((), (), s32[]{:S(2)}) async-start(), calls=%async_computation.8 | async-start | bytes 7077888 | tf_op jit(solution)/shard_map/all_gather | solution.py:65
  9.7 102.7 %all-gather.11.cloned.1.call-start = ((), (), s32[]{:S(2)}) async-start(), calls=%async_computation.10 | async-start | bytes 2621440 | tf_op jit(solution)/shard_map/all_gather | solution.py:100
  92.4 45.0 %all-gather.9.cloned.1.call-start = ((), (), s32[]{:S(2)}) async-start(), calls=%async_computation.9 | async-start | bytes 2621440 | tf_op jit(solution)/shard_map/all_gather | solution.py:101
  98.5 68.6 %all-gather.13.cloned.1.call-start = ((), (), s32[]{:S(2)}) async-start(), calls=%async_computation.11 | async-start | bytes 2359296 | tf_op jit(solution)/shard_map/all_gather | solution.py:66
  99.1 228.1 %all-reduce.7.cloned.1.call-start = ((), (), s32[]{:S(2)}) async-start(), calls=%async_computation.12 | async-start | bytes 8388608 | tf_op jit(solution)/shard_map/psum | solution.py:125
  172.1 245.9 %all-gather.17.cloned.1.call-start = ((), (), s32[]{:S(2)}) async-start(), calls=%async_computation.14 | async-start | bytes 18874368 | tf_op jit(solution)/shard_map/all_gather | solution.py:132
  172.6 408.2 %all-gather.15.cloned.1.call-start = ((), (), s32[]{:S(2)}) async-start(), calls=%async_computation.13 | async-start | bytes 37748736 | tf_op jit(solution)/shard_map/all_gather | solution.py:131
  173.4 1213.3 %all-reduce.11.cloned.1.call-start = ((), (), s32[]{:S(2)}) async-start(), calls=%async_computation.16 | async-start | bytes 8388608 | tf_op jit(solution)/shard_map/psum | solution.py:195
  1230.6 244.6 %all-reduce.9.cloned.1.call-start = ((), (), s32[]{:S(2)}) async-start(), calls=%async_computation.15 | async-start | bytes 4194304 | tf_op jit(solution)/shard_map/psum | solution.py:160
  1234.5 301.7 %reduce-scatter.13.cloned.1.call-start = ((), (), s32[]{:S(2)}) async-start(), calls=%async_computation.18 | async-start | bytes 5242880 | tf_op jit(solution)/shard_map/reduce_scatter | solution.py:245
  1492.6 90.7 %reduce-scatter.11.cloned.1.call-start = ((), (), s32[]{:S(2)}) async-start(), calls=%async_computation.17 | async-start | bytes 5242880 | tf_op jit(solution)/shard_map/reduce_scatter | solution.py:244
  1509.8 73.5 %copy-start.20 = (f32[256,64]{1,0:T(8,128)S(1)}, f32[256,64]{1,0:T(8,128)}, u32[]{:S(2)}) copy-start(f32[256,64]{1,0:T(8,128)} %copy-done.19) | copy-start | bytes 196612
  1509.8 73.5 %copy-start.22 = (f32[256,64]{1,0:T(8,128)S(1)}, f32[256,64]{1,0:T(8,128)}, u32[]{:S(2)}) copy-start(f32[256,64]{1,0:T(8,128)} %copy-done.21) | copy-start | bytes 196612
  1509.8 274.0 %all-reduce.13.cloned.1.call-start = ((), (), s32[]{:S(2)}) async-start(), calls=%async_computation.19 | async-start | bytes 8388608 | tf_op jit(solution)/shard_map/psum | solution.py:274
  1631.4 152.4 %copy-start.29 = (f32[1,2048]{1,0:T(1,128)S(1)}, f32[1,2048]{1,0:T(1,128)}, u32[]{:S(2)}) copy-start(f32[1,2048]{1,0:T(1,128)} %copy-done.28) | copy-start | bytes 24580
  1631.4 152.4 %copy-start.31 = (f32[1,2,2,128]{3,1,2,0:T(2,128)S(1)}, f32[1,2,2,128]{3,1,2,0:T(2,128)}, u32[]{:S(2)}) copy-start(f32[1,2,2,128]{3,1,2,0:T(2,128)} %copy-done.30) | copy-start | bytes 6148
  1631.4 158.3 %copy-start.24 = (bf16[1,512,512]{1,2,0:T(8,128)(2,1)S(1)}, bf16[1,512,512]{1,2,0:T(8,128)(2,1)}, u32[]{:S(2)}) copy-start(bf16[1,512,512]{1,2,0:T(8,128)(2,1)} %copy-done.23) | copy-start | bytes 1572868
  1631.4 158.3 %copy-start.26 = (bf16[1,512,512]{1,2,0:T(8,128)(2,1)S(1)}, bf16[1,512,512]{1,2,0:T(8,128)(2,1)}, u32[]{:S(2)}) copy-start(bf16[1,512,512]{1,2,0:T(8,128)(2,1)} %copy-done.25) | copy-start | bytes 1572868
  1631.5 193.0 %reduce-scatter.25.cloned.1.call-start = ((), (), s32[]{:S(2)}) async-start(), calls=%async_computation.25 | async-start | bytes 1179648
  1789.2 131.0 %reduce-scatter.15.cloned.1.call-start = ((), (), s32[]{:S(2)}) async-start(), calls=%async_computation.20 | async-start | bytes 14155776 | tf_op jit(solution)/shard_map/reduce_scatter | solution.py:283
  1799.5 157.5 %reduce-scatter.19.cloned.1.call-start = ((), (), s32[]{:S(2)}) async-start(), calls=%async_computation.22 | async-start | bytes 147456 | tf_op jit(solution)/shard_map/reduce_scatter | solution.py:205
  1800.6 211.9 %reduce-scatter.17.cloned.1.call-start = ((), (), s32[]{:S(2)}) async-start(), calls=%async_computation.21 | async-start | bytes 4718592 | tf_op jit(solution)/shard_map/reduce_scatter | solution.py:284
  1806.2 415.6 %reduce-scatter.23.cloned.1.call-start = ((), (), s32[]{:S(2)}) async-start(), calls=%async_computation.24 | async-start | bytes 37748736 | tf_op jit(solution)/shard_map/reduce_scatter | solution.py:204
  1806.8 803.2 %reduce-scatter.21.cloned.1.call-start = ((), (), s32[]{:S(2)}) async-start(), calls=%async_computation.23 | async-start | bytes 75497472 | tf_op jit(solution)/shard_map/reduce_scatter | solution.py:203
  (113 other events, 818.5 us)
Sparse Core Ops, SparseCore 0:
  10.5 49.3 all-gather.6
  92.6 19.8 all-gather.10
  114.6 22.8 all-gather.8
  139.2 27.8 all-gather.12
  172.2 154.9 all-reduce.6
  329.1 88.8 all-gather.16
  420.0 160.7 all-gather.14
  1230.7 155.9 all-reduce.10
  1389.7 85.5 all-reduce.8
  1492.8 43.4 reduce-scatter.12
  1538.8 44.5 reduce-scatter.10
  1631.6 152.2 all-reduce.12
  1789.3 35.0 reduce-scatter.24
  1827.8 92.3 reduce-scatter.14
  1923.6 33.3 reduce-scatter.18
  1961.1 51.3 reduce-scatter.16
  2016.5 205.2 reduce-scatter.22
  2226.2 383.7 reduce-scatter.20
where the time goes:
time: 2630 us; the launch traced here: 2620 us
  waiting for transfers between devices  1700 us (65%)
  matrix products  489 us (19%)
  local copies, waits for them, and re-layouts  282 us (11%)
  blocking collectives  70.5 us (3%)
  other arithmetic  54.7 us (2%)
    reduce_scatter x1, waiting for transfers between devices, body(): lax.psum_scatter(grad_gate_up, ('fsdp', 'ctx'), scatter_dimension=2, tile...  388 us
    reduce_scatter x1, waiting for transfers between devices, body(): lax.psum_scatter(grad_down_all, ('fsdp', 'ctx'), scatter_dimension=1, til...  209 us
    dynamic_update_slice x80, local copies, waits for them, and re-layouts, body(): lax.scan(expert_backward, zero_rows, back_inputs)  176 us
    all_gather x1, waiting for transfers between devices, body(): lax.all_gather(gate_up_weight, ('fsdp', 'ctx'), axis=2, tiled=True)  163 us
    psum x1, waiting for transfers between devices, body(): lax.psum((grad_normed_part, placed_gains), 'tp')  152 us
    psum x1, waiting for transfers between devices, body(): attn_total = lax.psum(contract_last(heads_out, out_full), 'tp')  144 us
    psum x1, waiting for transfers between devices, body(): expert_grad_norm, gate_grads = lax.psum((expert_part, grad_gates.T), 'tp')  132 us
    dot_general x16, matrix products, expert_backward(): jnp.einsum('ctf,cdf->td', grad_acts, pair_weights, preferred_element_type...  97.3 us
  transfers between devices with their start and end apart: 18, of which 18 were waited for; matrix products, arithmetic and copies ran while one was open for 3% of the time, Pallas kernels for 0%

commit v1 on v0

--- a/solution.py
+++ b/solution.py
@@ -6,6 +6,22 @@
 HEAD_DIM = 128
 EPSILON = 1e-05
 THETA = 10000.0
+
+
+def ring_gather(x, axis, dim):
+    ways, here, step = (lax.axis_size(axis), lax.axis_index(axis), x.shape[dim])
+    dims = [n * ways if d == dim else n for d, n in enumerate(x.shape)]
+    full = lax.dynamic_update_slice_in_dim(jnp.zeros(dims, x.dtype), x, here * step, axis=dim)
+    going_up = going_down = x
+    for far in range(1, ways // 2 + 1):
+        going_up = lax.ppermute(going_up, axis, [(d, (d + 1) % ways) for d in range(ways)])
+        full = lax.dynamic_update_slice_in_dim(full, going_up, (here - far) % ways * step, axis=dim)
+        if 2 * far < ways:
+            going_down = lax.ppermute(going_down, axis, [(d, (d - 1) % ways) for d in range(ways)])
+            full = lax.dynamic_update_slice_in_dim(
+                full, going_down, (here + far) % ways * step, axis=dim
+            )
+    return full
 
 
 def rotary_tables(positions, head_width):
@@ -129,7 +145,7 @@
     normed_two = (normal_two * gains[1]).astype(jnp.bfloat16)
     gate_up_full, down_full, router_full = (
         lax.all_gather(gate_up_weight, ("fsdp", "ctx"), axis=2, tiled=True),
-        lax.all_gather(down_weight, ("fsdp", "ctx"), axis=1, tiled=True),
+        ring_gather(down_weight, ("fsdp", "ctx"), 1),
         lax.all_gather(router_weight, ("fsdp", "ctx"), axis=0, tiled=True),
     )
     expert_count = router_full.shape[1]

time: 2630 us -> 2540 us (0.966)
  waiting for transfers between devices: 1700 us -> 1460 us
  starting transfers between devices: 1.97 us -> 109 us
  local copies, waits for them, and re-layouts: 282 us -> 309 us
    psum x1, waiting for transfers between devices: 144 us -> 0.01 us  [body(): attn_total = lax.psum(contract_last(heads_out, out_full), 'tp')]
    ppermute x0 -> x7, starting transfers between devices: none -> 107 us  [the longest x4 105 us: ring_gather(): lax.ppermute(going_up, axis, [(d, (d + 1) % ways) for d in range(ways)])]
    all_gather x1, waiting for transfers between devices: 86 us -> 0.01 us  [body(): lax.all_gather(down_weight, ('fsdp', 'ctx'), axis=1, tiled=True)]
    all_gather x1, waiting for transfers between devices: 163 us -> 113 us  [body(): lax.all_gather(gate_up_weight, ('fsdp', 'ctx'), axis=2, tiled=True)]
    ppermute x0 -> x7, waiting for transfers between devices: none -> 33.8 us  [the longest x4 33.8 us: ring_gather(): lax.ppermute(going_up, axis, [(d, (d + 1) % ways) for d in range(ways)])]
  transfers between devices with their start and end apart: 18 -> 25, of which waited for: 18 -> 19; matrix products, arithmetic and copies ran while one was open for 3% -> 9% of each run, Pallas kernels for 0% -> 0%
where the time goes in v1:
time: 2540 us; the launch traced here: 2530 us
  waiting for transfers between devices  1460 us (57%)
  matrix products  490 us (19%)
  local copies, waits for them, and re-layouts  309 us (12%)
  starting transfers between devices  109 us (4%)
  blocking collectives  92.6 us (4%)
  other arithmetic  54.7 us (2%)
    reduce_scatter x1, waiting for transfers between devices, body(): lax.psum_scatter(grad_gate_up, ('fsdp', 'ctx'), scatter_dimension=2, tile...  388 us
    reduce_scatter x1, waiting for transfers between devices, body(): lax.psum_scatter(grad_down_all, ('fsdp', 'ctx'), scatter_dimension=1, til...  209 us
    dynamic_update_slice x80, local copies, waits for them, and re-layouts, body(): lax.scan(expert_backward, zero_rows, back_inputs)  177 us
    psum x1, waiting for transfers between devices, body(): lax.psum((grad_normed_part, placed_gains), 'tp')  152 us
    psum x1, waiting for transfers between devices, body(): expert_grad_norm, gate_grads = lax.psum((expert_part, grad_gates.T), 'tp')  132 us
    all_gather x1, waiting for transfers between devices, body(): lax.all_gather(gate_up_weight, ('fsdp', 'ctx'), axis=2, tiled=True)  113 us
    ppermute x4, starting transfers between devices, ring_gather(): lax.ppermute(going_up, axis, [(d, (d + 1) % ways) for d in range(ways)])  105 us
    dot_general x16, matrix products, expert_backward(): jnp.einsum('ctf,cdf->td', grad_acts, pair_weights, preferred_element_type...  96.8 us
  transfers between devices with their start and end apart: 25, of which 19 were waited for; matrix products, arithmetic and copies ran while one was open for 9% of the time, Pallas kernels for 0%

profile of v1, /device:TPU:0, one launch (start us, length us, event | category | flops | bytes accessed | tf_op | source)
XLA Modules:
  0.0 2529.2 jit_solution(1386468456552333079)
XLA Ops:
  24.7 35.1 %all-gather.7.cloned.1.call-done = bf16[3,2048,512]{1,2,0:T(8,128)(2,1)} async-done(((bf16[3,256,512]{1,2,0:T(8,128)(2,1)}), bf16[3,2048,512]{1,2,0:T(8,128)(2,1)}) %all-gather.7.cloned.1.call-update) | async-done | bytes 6291472 | tf_op jit(solution)/shard_map/all_gather | solution.py:81
  100.7 11.8 all-gather.11.cloned.1.call-done
  121.5 16.0 all-gather.9.cloned.1.call-done
  143.6 23.5 all-gather.13.cloned.1.call-done
  176.2 24.0 collective-permute-done
  201.5 20.6 collective-permute-start.2
  228.0 40.3 %collective-permute-start.4 = (bf16[16,256,256]{2,1,0:T(8,128)(2,1)S(1)}, bf16[16,256,256]{2,1,0:T(8,128)(2,1)}, u32[]{:S(2)}, u32[]{:S(2)}) collective-permute-start(bf16[16,256,256]{2,1,0:T(8,128)(2,1)S(1)} %collective-permute-done.2), channel_id=1, source_target_pairs={{0,4},{4,8},{8,12},{12,16},{16,20},{20,24},{24,28},{28,0},{1,5},{5... | collective-permute-start | bytes 6291464 | tf_op jit(solution)/shard_map/ppermute | solution.py:17
  272.3 43.3 %collective-permute-start.6 = (bf16[16,256,256]{2,1,0:T(8,128)(2,1)}, bf16[16,256,256]{2,1,0:T(8,128)(2,1)}, u32[]{:S(2)}, u32[]{:S(2)}) collective-permute-start(bf16[16,256,256]{2,1,0:T(8,128)(2,1)} %collective-permute-done.4), channel_id=1, source_target_pairs={{0,4},{4,8},{8,12},{12,16},{16,20},{20,24},{24,28},{28,0},{1,5},{5... | collective-permute-start | bytes 6291464 | tf_op jit(solution)/shard_map/ppermute | solution.py:17
  315.6 30.8 %all_gather.31 = bf16[2048,16]{0,1:T(8,128)(2,1)S(1)} all-gather(bf16[256,16]{0,1:T(8,128)(2,1)S(1)} %copy-done.48), channel_id=1, replica_groups=mesh['fsdp'=2,'ctx'=4,'tp'=4] {'fsdp','ctx'}, dimensions={0}, use_global_device_ids=true | all-gather | bytes 73728 | tf_op jit(solution)/shard_map/all_gather | solution.py:149
  376.0 113.0 %all-gather.15.cloned.1.call-done = bf16[16,2,2048,256]{3,2,1,0:T(8,128)(2,1)} async-done(((bf16[16,2,256,256]{3,2,1,0:T(8,128)(2,1)}), bf16[16,2,2048,256]{3,2,1,0:T(8,128)(2,1)}) %all-gather.15.cloned.1.call-update) | async-done | bytes 33554448 | tf_op jit(solution)/shard_map/all_gather | solution.py:147
  489.0 147.4 %while.30 = (s32[]{:T(128)}, f32[512,2048]{1,0:T(8,128)}, f32[16,2,512,256]{2,3,1,0:T(8,128)}, f32[16,512]{1,0:T(8,128)S(1)}, bf16[16,2,2048,256]{3,2,1,0:T(8,12...) while((s32[]{:T(128)}, f32[512,2048]{1,0:T(8,128)}, ...), condition=%wide.region_13.14_spmd.clone, body=%wide.region_12.13_spmd.clone.sunk | while | flops 1613627392 | bytes 50338988 | solution.py:173
  636.3 505.4 %while.31 = (s32[]{:T(128)}, f32[512,2048]{1,0:T(8,128)}, f32[16,2,2048,256]{3,2,1,0:T(8,128)}, f32[16,2048,256]{2,1,0:T(8,128)}, f32[16,512]{1,0:T(8,128)S(1)},...) while((s32[]{:T(128)}, f32[512,2048]{1,0:T(8,128)}, ...), condition=%wide.region_17.18_spmd.clone, body=%wide.region_15.17_spmd.clone.sunk | while | flops 3226992128 | bytes 86523664 | solution.py:208
  1146.1 20.8 psum.75
  1167.0 131.9 %all-reduce.11.cloned.1.call-done = f32[512,2048]{1,0:T(8,128)} async-done(((f32[512,2048]{1,0:T(8,128)}), f32[512,2048]{1,0:T(8,128)}) %all-reduce.11.cloned.1.call-update) | async-done | bytes 4194320 | tf_op jit(solution)/shard_map/psum | solution.py:211
  1305.6 81.8 %all-reduce.9.cloned.1.call-done = bf16[512,2048]{1,0:T(8,128)(2,1)} async-done(((bf16[512,2048]{1,0:T(8,128)(2,1)}), bf16[512,2048]{1,0:T(8,128)(2,1)}) %all-reduce.9.cloned.1.call-update) | async-done | bytes 2097168 | tf_op jit(solution)/shard_map/psum | solution.py:176
  1426.7 21.7 reduce-scatter.13.cloned.1.call-done
  1453.3 42.3 %reduce-scatter.11.cloned.1.call-done = f32[2,256,4,128]{3,1,2,0:T(8,128)} async-done(((f32[2,1024,4,128]{3,1,2,0:T(8,128)}), f32[2,256,4,128]{3,1,2,0:T(8,128)}) %reduce-scatter.11.cloned.1.call-update) | async-done | bytes 1048592 | tf_op jit(solution)/shard_map/reduce_scatter | solution.py:260
  1513.6 18.9 all-reduce
  1543.7 152.4 %all-reduce.13.cloned.1.call-done = f32[512,2048]{1,0:T(8,128)} async-done(((f32[512,2048]{1,0:T(8,128)}), f32[512,2048]{1,0:T(8,128)}) %all-reduce.13.cloned.1.call-update) | async-done | bytes 4194320 | tf_op jit(solution)/shard_map/psum | solution.py:290
  1738.2 94.2 %reduce-scatter.15.cloned.1.call-done = f32[3,256,512]{1,2,0:T(8,128)} async-done(((f32[3,2048,512]{1,2,0:T(8,128)}), f32[3,256,512]{1,2,0:T(8,128)}) %reduce-scatter.15.cloned.1.call-update) | async-done | bytes 1572880 | tf_op jit(solution)/shard_map/reduce_scatter | solution.py:299
  1835.4 33.8 %reduce-scatter.19.cloned.1.call-done = f32[256,16]{0,1:T(8,128)} async-done(((f32[2048,16]{0,1:T(8,128)}), f32[256,16]{0,1:T(8,128)}) %reduce-scatter.19.cloned.1.call-update) | async-done | bytes 16400 | tf_op jit(solution)/shard_map/reduce_scatter | solution.py:221
  1869.2 55.5 %reduce-scatter.17.cloned.1.call-done = f32[256,512]{1,0:T(8,128)} async-done(((f32[2048,512]{1,0:T(8,128)}), f32[256,512]{1,0:T(8,128)}) %reduce-scatter.17.cloned.1.call-update) | async-done | bytes 524304 | tf_op jit(solution)/shard_map/reduce_scatter | solution.py:300
  1924.7 209.3 %reduce-scatter.23.cloned.1.call-done = f32[16,256,256]{2,1,0:T(8,128)} async-done(((f32[16,2048,256]{2,1,0:T(8,128)}), f32[16,256,256]{2,1,0:T(8,128)}) %reduce-scatter.23.cloned.1.call-update) | async-done | bytes 4194320 | tf_op jit(solution)/shard_map/reduce_scatter | solution.py:220
  2134.0 388.2 %reduce-scatter.21.cloned.1.call-done = f32[16,2,256,256]{3,2,1,0:T(8,128)} async-done(((f32[16,2,2048,256]{3,2,1,0:T(8,128)}), f32[16,2,256,256]{3,2,1,0:T(8,128)}) %reduce-scatter.21.cloned.1.call-update) | async-done | bytes 8388624 | tf_op jit(solution)/shard_map/reduce_scatter | solution.py:219
  (609 shorter events, 903.7 us)
Async XLA Ops:
  7.2 52.7 %all-gather.7.cloned.1.call-start = ((), (), s32[]{:S(2)}) async-start(), calls=%async_computation.8 | async-start | bytes 7077888 | tf_op jit(solution)/shard_map/all_gather | solution.py:81
  9.7 102.8 %all-gather.11.cloned.1.call-start = ((), (), s32[]{:S(2)}) async-start(), calls=%async_computation.10 | async-start | bytes 2621440 | tf_op jit(solution)/shard_map/all_gather | solution.py:116
  92.5 45.0 %all-gather.9.cloned.1.call-start = ((), (), s32[]{:S(2)}) async-start(), calls=%async_computation.9 | async-start | bytes 2621440 | tf_op jit(solution)/shard_map/all_gather | solution.py:117
  98.6 68.6 %all-gather.13.cloned.1.call-start = ((), (), s32[]{:S(2)}) async-start(), calls=%async_computation.11 | async-start | bytes 2359296 | tf_op jit(solution)/shard_map/all_gather | solution.py:82
  99.1 272.0 %all-reduce.7.cloned.1.call-start = ((), (), s32[]{:S(2)}) async-start(), calls=%async_computation.12 | async-start | bytes 8388608 | tf_op jit(solution)/shard_map/psum | solution.py:141
  172.1 316.9 %all-gather.15.cloned.1.call-start = ((), (), s32[]{:S(2)}) async-start(), calls=%async_computation.13 | async-start | bytes 37748736 | tf_op jit(solution)/shard_map/all_gather | solution.py:147
  172.7 463.6 %all-gather.17.cloned.1.call-start = ((), (), s32[]{:S(2)}) async-start(), calls=%async_computation.15 | async-start | bytes 18874368 | tf_op jit(solution)/shard_map/all_gather | solution.py:182
  173.4 1125.5 %all-reduce.11.cloned.1.call-start = ((), (), s32[]{:S(2)}) async-start(), calls=%async_computation.16 | async-start | bytes 8388608 | tf_op jit(solution)/shard_map/psum | solution.py:211
  173.5 26.7 %collective-permute-start = (bf16[16,256,256]{2,1,0:T(8,128)(2,1)}, bf16[16,256,256]{2,1,0:T(8,128)(2,1)S(1)}, u32[]{:S(2)}, u32[]{:S(2)}) collective-permute-start(bf16[16,256,256]{2,1,0:T(8,128)(2,1)} %param.22), channel_id=1, source_target_pairs={{0,4},{4,8},{8,12},{12,16},{16,20},{20,24},{24,28},{28,0},{1,5},{5... | collective-permute-start | bytes 6291464 | tf_op jit(solution)/shard_map/ppermute | solution.py:17
  173.8 48.3 %collective-permute-start.1 = (bf16[16,256,256]{2,1,0:T(8,128)(2,1)}, bf16[16,256,256]{2,1,0:T(8,128)(2,1)S(1)}, u32[]{:S(2)}, u32[]{:S(2)}) collective-permute-start(bf16[16,256,256]{2,1,0:T(8,128)(2,1)} %param.22), channel_id=1, source_target_pairs={{0,28},{4,0},{8,4},{12,8},{16,12},{20,16},{24,20},{28,24},{1,29},{... | collective-permute-start | bytes 6291464 | tf_op jit(solution)/shard_map/ppermute | solution.py:20
  222.1 46.2 %collective-permute-start.3 = (bf16[16,256,256]{2,1,0:T(8,128)(2,1)S(1)}, bf16[16,256,256]{2,1,0:T(8,128)(2,1)}, u32[]{:S(2)}, u32[]{:S(2)}) collective-permute-start(bf16[16,256,256]{2,1,0:T(8,128)(2,1)S(1)} %collective-permute-done.1), channel_id=1, source_target_pairs={{0,28},{4,0},{8,4},{12,8},{16,12},{20,16},{24,20},{28,24},{1,29},{... | collective-permute-start | bytes 6291464 | tf_op jit(solution)/shard_map/ppermute | solution.py:20
  228.0 44.3 %collective-permute-start.4 = (bf16[16,256,256]{2,1,0:T(8,128)(2,1)S(1)}, bf16[16,256,256]{2,1,0:T(8,128)(2,1)}, u32[]{:S(2)}, u32[]{:S(2)}) collective-permute-start(bf16[16,256,256]{2,1,0:T(8,128)(2,1)S(1)} %collective-permute-done.2), channel_id=1, source_target_pairs={{0,4},{4,8},{8,12},{12,16},{16,20},{20,24},{24,28},{28,0},{1,5},{5... | collective-permute-start | bytes 6291464 | tf_op jit(solution)/shard_map/ppermute | solution.py:17
  268.4 96.6 %collective-permute-start.5 = (bf16[16,256,256]{2,1,0:T(8,128)(2,1)}, bf16[16,256,256]{2,1,0:T(8,128)(2,1)}, u32[]{:S(2)}, u32[]{:S(2)}) collective-permute-start(bf16[16,256,256]{2,1,0:T(8,128)(2,1)} %collective-permute-done.3), channel_id=1, source_target_pairs={{0,28},{4,0},{8,4},{12,8},{16,12},{20,16},{24,20},{28,24},{1,29},{... | collective-permute-start | bytes 6291464 | tf_op jit(solution)/shard_map/ppermute | solution.py:20
  272.3 95.8 %collective-permute-start.6 = (bf16[16,256,256]{2,1,0:T(8,128)(2,1)}, bf16[16,256,256]{2,1,0:T(8,128)(2,1)}, u32[]{:S(2)}, u32[]{:S(2)}) collective-permute-start(bf16[16,256,256]{2,1,0:T(8,128)(2,1)} %collective-permute-done.4), channel_id=1, source_target_pairs={{0,4},{4,8},{8,12},{12,16},{16,20},{20,24},{24,28},{28,0},{1,5},{5... | collective-permute-start | bytes 6291464 | tf_op jit(solution)/shard_map/ppermute | solution.py:17
  1141.7 245.7 %all-reduce.9.cloned.1.call-start = ((), (), s32[]{:S(2)}) async-start(), calls=%async_computation.14 | async-start | bytes 4194304 | tf_op jit(solution)/shard_map/psum | solution.py:176
  1145.6 302.8 %reduce-scatter.13.cloned.1.call-start = ((), (), s32[]{:S(2)}) async-start(), calls=%async_computation.18 | async-start | bytes 5242880 | tf_op jit(solution)/shard_map/reduce_scatter | solution.py:261
  1404.8 90.7 %reduce-scatter.11.cloned.1.call-start = ((), (), s32[]{:S(2)}) async-start(), calls=%async_computation.17 | async-start | bytes 5242880 | tf_op jit(solution)/shard_map/reduce_scatter | solution.py:260
  1422.0 274.0 %all-reduce.13.cloned.1.call-start = ((), (), s32[]{:S(2)}) async-start(), calls=%async_computation.19 | async-start | bytes 8388608 | tf_op jit(solution)/shard_map/psum | solution.py:290
  1543.6 193.0 %reduce-scatter.25.cloned.1.call-start = ((), (), s32[]{:S(2)}) async-start(), calls=%async_computation.25 | async-start | bytes 1179648
  1701.4 131.0 %reduce-scatter.15.cloned.1.call-start = ((), (), s32[]{:S(2)}) async-start(), calls=%async_computation.20 | async-start | bytes 14155776 | tf_op jit(solution)/shard_map/reduce_scatter | solution.py:299
  1711.5 157.7 %reduce-scatter.19.cloned.1.call-start = ((), (), s32[]{:S(2)}) async-start(), calls=%async_computation.22 | async-start | bytes 147456 | tf_op jit(solution)/shard_map/reduce_scatter | solution.py:221
  1712.6 212.1 %reduce-scatter.17.cloned.1.call-start = ((), (), s32[]{:S(2)}) async-start(), calls=%async_computation.21 | async-start | bytes 4718592 | tf_op jit(solution)/shard_map/reduce_scatter | solution.py:300
  1718.2 415.8 %reduce-scatter.23.cloned.1.call-start = ((), (), s32[]{:S(2)}) async-start(), calls=%async_computation.24 | async-start | bytes 37748736 | tf_op jit(solution)/shard_map/reduce_scatter | solution.py:220
  1718.8 803.4 %reduce-scatter.21.cloned.1.call-start = ((), (), s32[]{:S(2)}) async-start(), calls=%async_computation.23 | async-start | bytes 75497472 | tf_op jit(solution)/shard_map/reduce_scatter | solution.py:219
  (127 other events, 1982.5 us)
Sparse Core Ops, SparseCore 0:
  10.5 49.3 all-gather.6
  92.6 19.8 all-gather.10
  114.6 22.8 all-gather.8
  139.2 27.8 all-gather.12
  172.2 154.9 all-reduce.6
  329.1 159.7 all-gather.14
  491.0 89.8 all-gather.16
  1141.9 157.0 all-reduce.10
  1301.9 85.5 all-reduce.8
  1405.0 43.4 reduce-scatter.12
  1451.0 44.5 reduce-scatter.10
  1543.7 152.2 all-reduce.12
  1701.5 35.0 reduce-scatter.24
  1740.0 92.3 reduce-scatter.14
  1835.8 33.3 reduce-scatter.18
  1873.3 51.3 reduce-scatter.16
  1928.7 205.2 reduce-scatter.22
  2138.4 383.7 reduce-scatter.20
